TPU v7x, 32 devices: a whole 2x2x4 slice. The times are simulated.
32 devices in a mesh: seq: 8 (over z, core), head: 4 (over y, x).
Axes of the slice: x: 2, y: 2, z: 4, core: 2. Of those that a mesh axis runs over, the one named last changes fastest.
Arguments:
- inputs: float32 [8192, 5120], P(('seq', 'head')), may hold values from -6 to 6
- log_decay: float32 [8192, 80], P(('seq', 'head')), may hold values from -1 to 0
- input_map: float32 [8192, 128], P(('seq', 'head')), may hold values from -0.31533617 to 0.31533617
- output_map: float32 [8192, 128], P(('seq', 'head')), may hold values from -0.31533617 to 0.31533617
- skip_gain: float32 [80], replicated, may hold values from 0.5 to 2
Outputs:
- outputs: float32 [8192, 5120], P(('seq', 'head'))
All inputs are finite; a program needn't handle non-finite values.
Results may differ from a plain program's by a relative error of at most 0.0001.
Values sent between devices are 32-bit elements; how exact they have to be, the bound alone decides.
A program may use at most 128 MiB of HBM per device.

v0:
```python
import jax
import jax.numpy as jnp
from jax import lax
from jax.sharding import PartitionSpec as P

BLOCK = 128


PRECISE = lax.Precision.HIGHEST


def from_behind(value, axis, steps):
    count = lax.axis_size(axis)
    leading, last = (max(0, -steps), min(count, count - steps))
    return lax.ppermute(value, axis, [(source, source + steps) for source in range(leading, last)])


def scan_blocks(inputs, log_decay, input_map, output_map, head_dim):
    token_count = inputs.shape[0]
    width = inputs.shape[1]
    head_count = log_decay.shape[1]
    state_width = input_map.shape[1]
    blocks = token_count // BLOCK
    x_all = inputs.reshape(blocks, BLOCK, width)
    d_all = log_decay.reshape(blocks, BLOCK, head_count)
    b_all = input_map.reshape(blocks, BLOCK, state_width)
    c_all = output_map.reshape(blocks, BLOCK, state_width)
    running = jnp.cumsum(d_all, axis=1)
    run_heads = jnp.moveaxis(running, 2, 1)
    positions = jnp.arange(BLOCK)
    causal = positions[:, None] >= positions[None, :]
    spread = run_heads[:, :, :, None] - run_heads[:, :, None, :]
    decays = jnp.where(causal[None, None], jnp.exp(jnp.minimum(spread, 0.0)), 0.0)
    scores = jnp.einsum("bin,bjn->bij", c_all, b_all, precision=PRECISE)
    weighted = scores[:, None] * decays
    per_head = x_all.reshape(blocks, BLOCK, head_count, head_dim)
    within = jnp.einsum("bhij,bjhp->bihp", weighted, per_head, precision=PRECISE).reshape(
        blocks, BLOCK, width
    )
    closing = running[:, -1, :]
    remains = jnp.repeat(jnp.exp(closing[:, None, :] - running), head_dim, axis=2)
    own_state = jnp.einsum("bln,blw->bnw", b_all, x_all * remains, precision=PRECISE)
    totals = jnp.cumsum(closing, axis=0)
    before_total = totals - closing
    order = jnp.arange(blocks)
    earlier = order[:, None] > order[None, :]
    gap = before_total[:, None, :] - totals[None, :, :]
    link = jnp.where(earlier[:, :, None], jnp.exp(jnp.minimum(gap, 0.0)), 0.0)
    link_wide = jnp.repeat(link, head_dim, axis=2)
    entering = jnp.einsum("kjw,jnw->knw", link_wide, own_state, precision=PRECISE)
    final_weight = jnp.repeat(jnp.exp(totals[-1][None, :] - totals), head_dim, axis=1)
    memory = jnp.einsum("jw,jnw->nw", final_weight, own_state, precision=PRECISE)
    growth = jnp.repeat(jnp.exp(running), head_dim, axis=2)
    carried = jnp.einsum("bin,bnw->biw", c_all, entering, precision=PRECISE) * growth
    prefix = running + before_total[:, None, :]
    return (
        (within + carried).reshape(token_count, width),
        prefix.reshape(token_count, head_count),
        memory,
        totals[-1],
    )


def shard_chain(summed, memory, head_dim):
    factor = jnp.repeat(jnp.exp(summed), head_dim)[None, :]

    def advance(turn, incoming):
        return from_behind(factor * incoming + memory, "seq", 1)

    return lax.fori_loop(0, lax.axis_size("seq") - 1, advance, jnp.zeros_like(memory))


def on_device(inputs, log_decay, input_map, output_map, skip_gain):
    head_count = skip_gain.shape[0]
    head_dim = inputs.shape[1] // head_count
    state_width = input_map.shape[1]
    groups = lax.axis_size("head")
    local_heads = head_count // groups
    local_width = local_heads * head_dim
    results, prefix, memory, summed = scan_blocks(
        inputs, log_decay, input_map, output_map, head_dim
    )
    got_sum, got_state = (
        lax.all_to_all(
            summed.reshape(1, groups, local_heads), "head", split_axis=1, concat_axis=1, tiled=True
        ),
        lax.all_to_all(
            memory.reshape(state_width, groups, local_width),
            "head",
            split_axis=1,
            concat_axis=1,
            tiled=True,
        ),
    )

    def within_shard(carry, item):
        total_decay, total_state = carry
        decay_here, state_here = item
        scale_now = jnp.repeat(jnp.exp(decay_here), head_dim)[None, :]
        return ((total_decay + decay_here, scale_now * total_state + state_here), carry)

    start_carry = (
        jnp.zeros((local_heads,), jnp.float32),
        jnp.zeros((state_width, local_width), jnp.float32),
    )
    (shard_decay, shard_state), (before_decay, before_state) = lax.scan(
        within_shard, start_carry, (got_sum[0], jnp.moveaxis(got_state, 1, 0))
    )
    incoming = shard_chain(shard_decay, shard_state, head_dim)
    per_source = (
        jnp.repeat(jnp.exp(before_decay), head_dim, axis=1)[:, None, :] * incoming[None]
        + before_state
    )
    back = lax.all_to_all(
        jnp.moveaxis(per_source, 0, 1), "head", split_axis=1, concat_axis=1, tiled=True
    )
    arrived = back.reshape(state_width, head_count * head_dim)
    returned = results + jnp.dot(output_map, arrived, precision=PRECISE) * jnp.repeat(
        jnp.exp(prefix), head_dim, axis=1
    )
    return returned + inputs * jnp.repeat(skip_gain, head_dim)[None, :]


def solution(mesh):
    in_specs = (
        P(("seq", "head"), None),
        P(("seq", "head"), None),
        P(("seq", "head"), None),
        P(("seq", "head"), None),
        P(),
    )
    out_specs = P(("seq", "head"), None)
    return jax.shard_map(
        on_device, mesh=mesh, in_specs=in_specs, out_specs=out_specs, check_vma=False
    )
```

profile of v0, /device:TPU:10, one launch (start us, length us, event | category | flops | bytes accessed | tf_op | source)
XLA Modules:
  0.0 314.4 jit_solution(636426769772568378)
XLA Ops:
  6.3 5.9 %copy.40 = f32[2,128,5120]{1,2,0:T(8,128)} copy(f32[2,128,5120]{2,1,0:T(8,128)} %bitcast.78) | data formatting | bytes 10485760 | tf_op jit(solution)/shard_map/reshape | solution.py:24
  15.3 5.2 %convolution_bitcast_fusion.2 = f32[2,128,5120]{1,2,0:T(8,128)S(1)} fusion(f32[2,128,5120]{1,2,0:T(8,128)S(1)} %bitcast_multiply_fusion, f32[2,128,128]{2,1,0:T(8,128)S(1)} %bitcast.93), kind=kOutput, calls=%fused_computation.26 | convolution fusion | flops 2013265920 | bytes 10616832 | tf_op jit(solution)/shard_map/bln,blw->bnw/dot_general | solution.py:42
  22.9 50.3 %fusion.24 = f32[5120,1,128]{2,1,0:T(1,128)} fusion(f32[2,5120,1]{0,2,1:T(1,128)S(1)} %bitcast.89, f32[2,128,5120]{1,2,0:T(8,128)S(1)} %convolution_bitcast_fusion.2), kind=kOutput, calls=%fused_computation.34 | convolution fusion | flops 15728640 | bytes 7905280 | tf_op jit(solution)/shard_map/jw,jnw->nw/dot_general | solution.py:52
  73.2 4.6 %all-to-all-start.1 = ((f32[128,4,1280]{0,2,1:T(8,128)}), f32[128,4,1280]{0,2,1:T(8,128)}, u32[]{:S(2)}, u32[]{:S(2)}) async-start(f32[128,4,1280]{0,2,1:T(8,128)} %bitcast.24), calls=%async_computation.1 | async-start | bytes 5242880 | tf_op jit(solution)/shard_map/all_to_all | solution.py:87
  77.8 8.4 %reshape.93 = f32[2,128,80,64]{3,2,1,0:T(8,128)} reshape(f32[256,5120]{1,0:T(8,128)} %param.9) | data formatting | bytes 10485760 | tf_op jit(solution)/shard_map/reshape;reshape | solution.py:36
  86.1 5.9 %copy.53 = f32[256,5120]{0,1:T(8,128)} copy(f32[256,5120]{1,0:T(8,128)} %param.9) | data formatting | bytes 10485760 | tf_op args[0]
  92.5 24.9 %fusion.6 = f32[2,80,128,64]{2,3,1,0:T(8,128)} fusion(f32[2,128,80,64]{3,2,1,0:T(8,128)} %reshape.93, f32[2,80,128]{2,1,0:T(8,128)S(1)} %copy.35, f32[2,128,128]{2,1,0:T(8,128)S(1)} %fusion.32, pred[128,128]{1,0:T(8,128)(4,1)S(1)} %iota_compare_fusion), kind=kOutput, calls=%fused_computation.12 | convolution fusion | flops 2023751680 | bytes 10715136 | tf_op jit(solution)/shard_map/bhij,bjhp->bihp/dot_general | solution.py:37
  117.4 5.9 %copy.46 = f32[2,128,5120]{2,1,0:T(8,128)} copy(f32[2,128,5120]{1,2,0:T(8,128)} %bitcast.87) | data formatting | bytes 10485760 | tf_op jit(solution)/shard_map/reshape | solution.py:37
  126.1 6.0 %copy.45 = f32[2,128,5120]{2,1,0:T(8,128)} copy(f32[2,128,5120]{1,2,0:T(8,128)} %bitcast.84) | data formatting | bytes 10485760 | tf_op jit(solution)/shard_map/reshape | solution.py:53
  132.9 11.6 %while.29 = (s32[]{:T(128)}, f32[20]{0:T(128)S(1)}, f32[128,1280]{1,0:T(8,128)S(1)}, f32[4,20]{1,0:T(4,128)S(1)}, f32[4,128,1280]{1,2,0:T(8,128)}, /*index=5*/f3...) while((s32[]{:T(128)}, f32[20]{0:T(128)S(1)}, f32[128,1280]{1,0:T(8,128)S(1)}, ...), condition=%wide.region_3.4_spmd.clone, body=%wide.region_2.3_spmd.clone.sunk | while | flops 491563 | bytes 7885568 | solution.py:106
  144.6 84.9 %while.28 = (s32[]{:T(128)}, f32[128,1280]{1,0:T(8,128)S(1)}, f32[128,1280]{1,0:T(8,128)S(1)}, f32[20]{0:T(128)S(1)}, s32[]{:T(128)}) while((s32[]{:T(128)}, f32[128,1280]{1,0:T(8,128)S(1)}, f32[128,1280]{1,0:T(8,128)S(1)}, f32[20]{0:T(128)S(1)}, s32[]{:T(128)}) %tuple.53), condition=%wide.region_5.6_spmd.clone, body=%wide.region_4.5_spmd.clone.sunk | while | flops 327682 | bytes 4608181 | solution.py:70
  146.8 10.0 %collective-permute-done = f32[128,1280]{1,0:T(8,128)S(1)} collective-permute-done((f32[128,1280]{1,0:T(8,128)S(1)}, f32[128,1280]{1,0:T(8,128)S(1)}, u32[]{:S(2)}, u32[]{:S(2)}) %collective-permute-start) | collective-permute-done | bytes 655392 | tf_op jit(solution)/shard_map/while/body/eval_jaxpr/ppermute | solution.py:15
  158.9 10.0 %collective-permute-done = f32[128,1280]{1,0:T(8,128)S(1)} collective-permute-done((f32[128,1280]{1,0:T(8,128)S(1)}, f32[128,1280]{1,0:T(8,128)S(1)}, u32[]{:S(2)}, u32[]{:S(2)}) %collective-permute-start) | collective-permute-done | bytes 655392 | tf_op jit(solution)/shard_map/while/body/eval_jaxpr/ppermute | solution.py:15
  171.0 10.0 %collective-permute-done = f32[128,1280]{1,0:T(8,128)S(1)} collective-permute-done((f32[128,1280]{1,0:T(8,128)S(1)}, f32[128,1280]{1,0:T(8,128)S(1)}, u32[]{:S(2)}, u32[]{:S(2)}) %collective-permute-start) | collective-permute-done | bytes 655392 | tf_op jit(solution)/shard_map/while/body/eval_jaxpr/ppermute | solution.py:15
  183.1 10.0 %collective-permute-done = f32[128,1280]{1,0:T(8,128)S(1)} collective-permute-done((f32[128,1280]{1,0:T(8,128)S(1)}, f32[128,1280]{1,0:T(8,128)S(1)}, u32[]{:S(2)}, u32[]{:S(2)}) %collective-permute-start) | collective-permute-done | bytes 655392 | tf_op jit(solution)/shard_map/while/body/eval_jaxpr/ppermute | solution.py:15
  195.3 10.0 %collective-permute-done = f32[128,1280]{1,0:T(8,128)S(1)} collective-permute-done((f32[128,1280]{1,0:T(8,128)S(1)}, f32[128,1280]{1,0:T(8,128)S(1)}, u32[]{:S(2)}, u32[]{:S(2)}) %collective-permute-start) | collective-permute-done | bytes 655392 | tf_op jit(solution)/shard_map/while/body/eval_jaxpr/ppermute | solution.py:15
  207.4 10.0 %collective-permute-done = f32[128,1280]{1,0:T(8,128)S(1)} collective-permute-done((f32[128,1280]{1,0:T(8,128)S(1)}, f32[128,1280]{1,0:T(8,128)S(1)}, u32[]{:S(2)}, u32[]{:S(2)}) %collective-permute-start) | collective-permute-done | bytes 655392 | tf_op jit(solution)/shard_map/while/body/eval_jaxpr/ppermute | solution.py:15
  219.5 10.0 %collective-permute-done = f32[128,1280]{1,0:T(8,128)S(1)} collective-permute-done((f32[128,1280]{1,0:T(8,128)S(1)}, f32[128,1280]{1,0:T(8,128)S(1)}, u32[]{:S(2)}, u32[]{:S(2)}) %collective-permute-start) | collective-permute-done | bytes 655392 | tf_op jit(solution)/shard_map/while/body/eval_jaxpr/ppermute | solution.py:15
  233.1 4.3 %all-to-all-start.2 = ((f32[128,4,1280]{0,2,1:T(8,128)}), f32[128,4,1280]{0,2,1:T(8,128)S(1)}, u32[]{:S(2)}, u32[]{:S(2)}) async-start(f32[128,4,1280]{0,2,1:T(8,128)} %add_bitcast_fusion), calls=%async_computation.2 | async-start | bytes 5242880 | tf_op jit(solution)/shard_map/all_to_all | solution.py:114
  238.8 45.4 %fusion.28 = f32[2,128,5120]{1,0,2:T(2,128)S(1)} fusion(f32[2,2,5120]{1,0,2:T(2,128)S(1)} %bitcast.88, f32[2,128,5120]{1,2,0:T(8,128)} %copy-done.2), kind=kOutput, calls=%fused_computation.38 | convolution fusion | flops 31457280 | bytes 10567680 | tf_op jit(solution)/shard_map/kjw,jnw->knw/dot_general | solution.py:50
  284.3 7.0 %fusion.17 = f32[2,128,5120]{2,1,0:T(8,128)} fusion(f32[2,128,5120]{2,1,0:T(8,128)S(1)} %bitcast.80, f32[2,128,5120]{2,1,0:T(8,128)S(1)} %bitcast.82, f32[2,128,128]{2,1,0:T(8,128)S(1)} %bitcast.77, f32[2,128,5120]{1,0,2:T(2,128)S(1)} %fusion.28), kind=kOutput, calls=%fused_computation.25 | convolution fusion | flops 2015887360 | bytes 21102592 | tf_op jit(solution)/shard_map/bin,bnw->biw/dot_general | solution.py:54
  291.3 5.9 %copy.52 = f32[256,5120]{0,1:T(8,128)} copy(f32[256,5120]{1,0:T(8,128)} %bitcast.83) | data formatting | bytes 10485760 | tf_op jit(solution)/shard_map/reshape | solution.py:57
  300.0 8.3 %fusion.15 = f32[256,5120]{0,1:T(8,128)} fusion(f32[256,5120]{0,1:T(8,128)S(1)} %copy-done.1, f32[256,5120]{0,1:T(8,128)S(1)} %bitcast.85, f32[128,5120]{0,1:T(8,128)S(1)} %bitcast.86, f32[256,128]{1,0:T(8,128)S(1)} %copy-done, f32[256,5120]{0,1:T(8,128)} %copy.53, f32[5120]{0:T(1024)S(1)} %mul.71), kind=kOutput, calls=%fused_computation.22 | convolution fusion | flops 2018508800 | bytes 23744512 | tf_op jit(solution)/shard_map/dot_general | solution.py:118
  308.3 5.9 %copy.54 = f32[256,5120]{1,0:T(8,128)} copy(f32[256,5120]{0,1:T(8,128)} %fusion.15) | data formatting | bytes 10485760 | tf_op jit(solution)/shard_map/add | solution.py:121
  (127 shorter events, 50.0 us)
Async XLA Ops:
  0.0 92.2 %copy-start = (f32[256,128]{1,0:T(8,128)S(1)}, f32[256,128]{1,0:T(8,128)}, u32[]{:S(2)}) copy-start(f32[256,128]{1,0:T(8,128)} %param.12) | copy-start | bytes 393220
  2.0 71.2 %all-to-all-start = ((f32[1,4,20]{2,0,1:T(1,128)}), f32[1,4,20]{2,0,1:T(1,128)S(1)}, u32[]{:S(2)}, u32[]{:S(2)}) async-start(f32[1,4,20]{2,0,1:T(1,128)} %bitcast.17), calls=%async_computation | async-start | bytes 4096 | tf_op jit(solution)/shard_map/all_to_all | solution.py:84
  12.4 2.9 copy-start.3
  20.5 2.4 copy-start.2
  73.2 59.7 %all-to-all-start.1 = ((f32[128,4,1280]{0,2,1:T(8,128)}), f32[128,4,1280]{0,2,1:T(8,128)}, u32[]{:S(2)}, u32[]{:S(2)}) async-start(f32[128,4,1280]{0,2,1:T(8,128)} %bitcast.24), calls=%async_computation.1 | async-start | bytes 5242880 | tf_op jit(solution)/shard_map/all_to_all | solution.py:87
  144.8 11.9 %collective-permute-start = (f32[128,1280]{1,0:T(8,128)S(1)}, f32[128,1280]{1,0:T(8,128)S(1)}, u32[]{:S(2)}, u32[]{:S(2)}) collective-permute-start(f32[128,1280]{1,0:T(8,128)S(1)} %multiply_add_fusion.2), channel_id=1, source_target_pairs={{0,4},{4,8},{8,12},{12,16},{16,20},{20,24},{24,28},{1,5},{5,9},{9,... | collective-permute-start | bytes 1966088 | tf_op jit(solution)/shard_map/while/body/eval_jaxpr/ppermute | solution.py:15
  157.0 11.9 %collective-permute-start = (f32[128,1280]{1,0:T(8,128)S(1)}, f32[128,1280]{1,0:T(8,128)S(1)}, u32[]{:S(2)}, u32[]{:S(2)}) collective-permute-start(f32[128,1280]{1,0:T(8,128)S(1)} %multiply_add_fusion.2), channel_id=1, source_target_pairs={{0,4},{4,8},{8,12},{12,16},{16,20},{20,24},{24,28},{1,5},{5,9},{9,... | collective-permute-start | bytes 1966088 | tf_op jit(solution)/shard_map/while/body/eval_jaxpr/ppermute | solution.py:15
  169.1 11.9 %collective-permute-start = (f32[128,1280]{1,0:T(8,128)S(1)}, f32[128,1280]{1,0:T(8,128)S(1)}, u32[]{:S(2)}, u32[]{:S(2)}) collective-permute-start(f32[128,1280]{1,0:T(8,128)S(1)} %multiply_add_fusion.2), channel_id=1, source_target_pairs={{0,4},{4,8},{8,12},{12,16},{16,20},{20,24},{24,28},{1,5},{5,9},{9,... | collective-permute-start | bytes 1966088 | tf_op jit(solution)/shard_map/while/body/eval_jaxpr/ppermute | solution.py:15
  181.2 11.9 %collective-permute-start = (f32[128,1280]{1,0:T(8,128)S(1)}, f32[128,1280]{1,0:T(8,128)S(1)}, u32[]{:S(2)}, u32[]{:S(2)}) collective-permute-start(f32[128,1280]{1,0:T(8,128)S(1)} %multiply_add_fusion.2), channel_id=1, source_target_pairs={{0,4},{4,8},{8,12},{12,16},{16,20},{20,24},{24,28},{1,5},{5,9},{9,... | collective-permute-start | bytes 1966088 | tf_op jit(solution)/shard_map/while/body/eval_jaxpr/ppermute | solution.py:15
  193.3 11.9 %collective-permute-start = (f32[128,1280]{1,0:T(8,128)S(1)}, f32[128,1280]{1,0:T(8,128)S(1)}, u32[]{:S(2)}, u32[]{:S(2)}) collective-permute-start(f32[128,1280]{1,0:T(8,128)S(1)} %multiply_add_fusion.2), channel_id=1, source_target_pairs={{0,4},{4,8},{8,12},{12,16},{16,20},{20,24},{24,28},{1,5},{5,9},{9,... | collective-permute-start | bytes 1966088 | tf_op jit(solution)/shard_map/while/body/eval_jaxpr/ppermute | solution.py:15
  205.5 11.9 %collective-permute-start = (f32[128,1280]{1,0:T(8,128)S(1)}, f32[128,1280]{1,0:T(8,128)S(1)}, u32[]{:S(2)}, u32[]{:S(2)}) collective-permute-start(f32[128,1280]{1,0:T(8,128)S(1)} %multiply_add_fusion.2), channel_id=1, source_target_pairs={{0,4},{4,8},{8,12},{12,16},{16,20},{20,24},{24,28},{1,5},{5,9},{9,... | collective-permute-start | bytes 1966088 | tf_op jit(solution)/shard_map/while/body/eval_jaxpr/ppermute | solution.py:15
  217.6 11.9 %collective-permute-start = (f32[128,1280]{1,0:T(8,128)S(1)}, f32[128,1280]{1,0:T(8,128)S(1)}, u32[]{:S(2)}, u32[]{:S(2)}) collective-permute-start(f32[128,1280]{1,0:T(8,128)S(1)} %multiply_add_fusion.2), channel_id=1, source_target_pairs={{0,4},{4,8},{8,12},{12,16},{16,20},{20,24},{24,28},{1,5},{5,9},{9,... | collective-permute-start | bytes 1966088 | tf_op jit(solution)/shard_map/while/body/eval_jaxpr/ppermute | solution.py:15
  233.1 4.3 %copy-start.4 = (f32[2,2,80]{1,0,2:T(2,128)S(1)}, f32[2,2,80]{1,0,2:T(2,128)}, u32[]{:S(2)}) copy-start(f32[2,2,80]{1,0,2:T(2,128)} %copy.66) | copy-start | bytes 3844
  233.1 64.3 %all-to-all-start.2 = ((f32[128,4,1280]{0,2,1:T(8,128)}), f32[128,4,1280]{0,2,1:T(8,128)S(1)}, u32[]{:S(2)}, u32[]{:S(2)}) async-start(f32[128,4,1280]{0,2,1:T(8,128)} %add_bitcast_fusion), calls=%async_computation.2 | async-start | bytes 5242880 | tf_op jit(solution)/shard_map/all_to_all | solution.py:114
  237.5 46.8 %slice-start = ((s8[5242880]{0:T(1024)(128)(4,1)}), s8[1048576]{0:T(1024)(128)(4,1)S(1)}, s32[]{:S(2)}) async-start(s8[5242880]{0:T(1024)(128)(4,1)} %bitcast.79), calls=%async_computation.3 | async-start | bytes 2097152
  237.5 46.8 %slice-start.2 = ((s8[5242880]{0:T(1024)(128)(4,1)}), s8[4194304]{0:T(1024)(128)(4,1)S(1)}, s32[]{:S(2)}) async-start(s8[5242880]{0:T(1024)(128)(4,1)} %bitcast.81), calls=%async_computation.5 | async-start | bytes 8388608
  238.8 45.5 %slice-start.1 = ((s8[5242880]{0:T(1024)(128)(4,1)}), s8[4194304]{0:T(1024)(128)(4,1)S(1)}, s32[]{:S(2)}) async-start(s8[5242880]{0:T(1024)(128)(4,1)} %bitcast.79), calls=%async_computation.4 | async-start | bytes 8388608
  238.8 45.5 %slice-start.3 = ((s8[5242880]{0:T(1024)(128)(4,1)}), s8[1048576]{0:T(1024)(128)(4,1)S(1)}, s32[]{:S(2)}) async-start(s8[5242880]{0:T(1024)(128)(4,1)} %bitcast.81), calls=%async_computation.6 | async-start | bytes 2097152
  291.3 6.0 %copy-start.5 = (f32[80]{0:T(128)S(1)}, f32[80]{0:T(128)}, u32[]{:S(2)}) copy-start(f32[80]{0:T(128)} %param.13) | copy-start | bytes 964
  297.5 2.5 copy-start.1
where the time goes:
time: 321 us; the launch traced here: 314 us
  matrix products  142 us (44%)
  waiting for transfers between devices  69.8 us (22%)
  local copies, waits for them, and re-layouts  67.9 us (21%)
  starting transfers between devices  26.6 us (8%)
  other arithmetic  7.84 us (2%)
    ppermute x7, waiting for transfers between devices, from_behind(): lax.ppermute(value, axis, [(source, source + steps) for source in range(l...  69.8 us
    dot_general x1, matrix products, scan_blocks(): jnp.einsum('jw,jnw->nw', final_weight, own_state, precision=PRECISE)  50.3 us
    dot_general x1, matrix products, scan_blocks(): jnp.einsum('kjw,jnw->knw', link_wide, own_state, precision=PRECISE)  45.4 us
    dot_general x1, matrix products, scan_blocks(): jnp.einsum('bhij,bjhp->bihp', weighted, per_head, precision=PRECISE)  24.9 us
    ppermute x7, starting transfers between devices, from_behind(): lax.ppermute(value, axis, [(source, source + steps) for source in range(l...  13.4 us
    unnamed x23, local copies, waits for them, and re-layouts  11 us
    another operation x1, local copies, waits for them, and re-layouts, scan_blocks(): per_head = x_all.reshape(blocks, BLOCK, head_count, head_dim)  8.36 us
    dot_general x1, matrix products, on_device(): jnp.dot(output_map, arrived, precision=PRECISE)  8.34 us
  transfers between devices with their start and end apart: 10, of which 7 were waited for; matrix products, arithmetic and copies ran while one was open for 57% of the time, Pallas kernels for 0%

commit v1 on v0

v1 whole, which is shorter than its diff:
```python
import functools

import jax
import jax.numpy as jnp
from jax import lax
from jax.experimental import pallas as pl
from jax.experimental.pallas import tpu as pltpu
from jax.sharding import PartitionSpec as P

BLOCK = 128
LANES = 128
PRECISE = lax.Precision.HIGHEST
MESH = pl.DeviceIdType.MESH
F32 = jnp.float32
BF16 = jnp.bfloat16


def split2(value):
    high = value.astype(BF16)
    return high, (value - high.astype(F32)).astype(BF16)


def split3(value):
    high = value.astype(BF16)
    rest = value - high.astype(F32)
    middle = rest.astype(BF16)
    return high, middle, (rest - middle.astype(F32)).astype(BF16)


def dot(a, b):
    return jnp.dot(a, b, preferred_element_type=F32)


def dot3(a_high, a_low, b):
    b_high, b_low = split2(b)
    return dot(a_high, b_high) + (dot(a_high, b_low) + dot(a_low, b_high))


def piece_plan(width, groups):
    units = width // LANES
    per_owner = -(-units // groups)
    wide = 2 if units == per_owner * groups and per_owner % 2 == 0 else 1
    return per_owner // wide, wide * LANES


def kernel(
    groups, shards, chunks, piece, head_dim,
    x_hbm, d_ref, b_ref, c_ref, gain_ref, out_hbm,
    x_s, out_s, go_s, m0_s, ms_s, r_s, ps_s, pr_s, hin_s, hout_s, bef_s, a_s, rows_s,
    l_hi, l_lo, cm_hi, cm_lo, gi_hi, gi_lo, gx_hi, gx_lo, row_a, row_b, row_c, tot_s, totr_s,
    x_sem, o_sem, ms_send, ms_recv, ps_send, ps_recv, h_send, h_recv, t_send, t_recv,
):
    seq = lax.axis_index("seq")
    me = lax.axis_index("head")
    tokens, width = x_hbm.shape
    heads = d_ref.shape[1]
    blocks = tokens // BLOCK
    state = b_ref.shape[1]
    exact = groups * chunks * piece == width

    def behind(d):
        return lax.rem(me - d + groups, groups)

    def ahead(d):
        return lax.rem(me + d, groups)

    def column(group, k):
        return (group * chunks + k) * piece

    def clamped(start):
        return pl.multiple_of(start if exact else jnp.minimum(start, width - piece), LANES)

    def one_hot(start, count):
        row = lax.broadcasted_iota(jnp.int32, (count, piece), 0)
        col = lax.broadcasted_iota(jnp.int32, (count, piece), 1)
        low = row * head_dim - start
        hit = jnp.logical_and(col >= low, col < low + head_dim)
        return jnp.where(hit, 1.0, 0.0).astype(BF16)

    def x_copy(k, d):
        start = clamped(column(ahead(d), k))
        return pltpu.make_async_copy(x_hbm.at[:, pl.ds(start, piece)], x_s.at[k, d], x_sem.at[k, d])

    def out_copy(k, d):
        start = clamped(column(ahead(d), k))
        return pltpu.make_async_copy(out_s.at[k, d], out_hbm.at[:, pl.ds(start, piece)], o_sem.at[k, d])

    def m_copy(k, d):
        return pltpu.make_async_remote_copy(
            src_ref=ms_s.at[k, d], dst_ref=r_s.at[k, d], send_sem=ms_send.at[k, d],
            recv_sem=ms_recv.at[k, d], device_id=(seq, ahead(d)), device_id_type=MESH)

    def p_copy(k, d):
        return pltpu.make_async_remote_copy(
            src_ref=ps_s.at[k, d], dst_ref=pr_s.at[k, d], send_sem=ps_send.at[k, d],
            recv_sem=ps_recv.at[k, d], device_id=(seq, ahead(d)), device_id_type=MESH)

    def h_copy(k):
        return pltpu.make_async_remote_copy(
            src_ref=hout_s.at[k], dst_ref=hin_s.at[k], send_sem=h_send.at[k],
            recv_sem=h_recv.at[k], device_id=(lax.rem(seq + 1, shards), me), device_id_type=MESH)

    def t_copy(d):
        return pltpu.make_async_remote_copy(
            src_ref=tot_s, dst_ref=totr_s.at[d], send_sem=t_send.at[d],
            recv_sem=t_recv.at[d], device_id=(seq, ahead(d)), device_id_type=MESH)

    barrier = pltpu.get_barrier_semaphore()
    for d in range(1, groups):
        pl.semaphore_signal(barrier, inc=1, device_id=(seq, ahead(d)), device_id_type=MESH)
    for step in (1, shards - 1):
        pl.semaphore_signal(
            barrier, inc=1, device_id=(lax.rem(seq + step, shards), me), device_id_type=MESH)

    @pl.loop(0, chunks * groups)
    def _(p):
        k = p // groups
        x_copy(k, lax.rem(p - k * groups + 1, groups)).start()

    rows = lax.broadcasted_iota(jnp.int32, (BLOCK, BLOCK), 0)
    cols = lax.broadcasted_iota(jnp.int32, (BLOCK, BLOCK), 1)
    causal = rows >= cols
    lower = jnp.where(causal, 1.0, 0.0).astype(F32)
    middles, ends = [], []
    for b in range(blocks):
        at = pl.ds(b * BLOCK, BLOCK)
        running = jnp.dot(lower, d_ref[at, :], precision=PRECISE, preferred_element_type=F32)
        middle = running[BLOCK // 2 - 1:BLOCK // 2, :]
        middles.append(middle)
        ends.append(running[BLOCK - 1:BLOCK, :])
        gi_hi[at, :], gi_lo[at, :] = split2(jnp.exp(middle - running))
        gx_hi[at, :], gx_lo[at, :] = split2(jnp.exp(running - middle))
        c_block, b_block = c_ref[at, :], b_ref[at, :]
        scores = lax.dot_general(
            c_block, b_block, (((1,), (1,)), ((), ())), precision=PRECISE, preferred_element_type=F32)
        stacked = jnp.concatenate([jnp.where(causal, scores, 0.0), b_block.T], axis=0)
        l_hi[b], l_lo[b] = split2(stacked)
        cm_hi[b], cm_lo[b] = split2(c_block)
    total = sum(ends[1:], ends[0])
    tot_s[...] = jnp.zeros_like(tot_s)
    tot_s[0:1, 0:heads] = total
    totr_s[0] = jnp.zeros_like(tot_s)
    totr_s[0, 0:1, 0:heads] = total
    small = jnp.concatenate(
        [jnp.exp(m) for m in middles] + [jnp.exp(e - m) for e, m in zip(ends, middles)]
        + [jnp.exp(e) for e in ends] + [gain_ref[...]], axis=0)
    count = small.shape[0]
    row_a[0:count, :], row_b[0:count, :], row_c[0:count, :] = split3(small)

    pl.semaphore_wait(barrier, groups + 1)
    for d in range(1, groups):
        t_copy(d).start()

    @pl.loop(0, chunks * groups)
    def _(p):
        k = p // groups
        d = lax.rem(p - k * groups + 1, groups)
        hot = one_hot(column(ahead(d), k), heads)
        grow_in = dot(gi_hi[...], hot) + dot(gi_lo[...], hot)
        grow_out = dot(gx_hi[...], hot) + dot(gx_lo[...], hot)
        wide = dot(row_a[...], hot) + (dot(row_b[...], hot) + dot(row_c[...], hot))
        go_s[k, d] = grow_out
        rows_s[k, d] = wide[0:rows_s.shape[2]]
        gain = wide[3 * blocks:3 * blocks + 1]
        x_copy(k, d).wait()
        memory = None
        for b in range(blocks):
            low, high = b * BLOCK, (b + 1) * BLOCK
            x = x_s[k, d, low:high, :]
            both = dot3(l_hi[b], l_lo[b], x * grow_in[low:high])
            out_s[k, d, low:high, :] = both[:BLOCK] * grow_out[low:high] + gain * x
            added = both[BLOCK:] * wide[blocks + b:blocks + b + 1]
            if b > 0:
                m0_s[k, d, b - 1] = memory
                memory = memory * wide[2 * blocks + b:2 * blocks + b + 1] + added
            else:
                memory = added

        @pl.when(d == 0)
        def _():
            r_s[k, 0] = memory

        @pl.when(d != 0)
        def _():
            ms_s[k, d] = memory
            m_copy(k, d).start()

    for d in range(1, groups):
        t_copy(d).wait_recv()

    @pl.loop(0, chunks)
    def _(k):
        hot = one_hot(column(me, k), LANES)
        factors = []
        for j in range(groups):
            parts = split3(jnp.exp(totr_s[behind(j)]))
            factors.append((dot(parts[0], hot) + (dot(parts[1], hot) + dot(parts[2], hot)))[0:1])
        for d in range(1, groups):
            m_copy(k, d).wait_recv()
        running = r_s[k, behind(0)]
        decay = factors[0]
        bef_s[0] = jnp.zeros_like(running)
        a_s[0] = jnp.ones_like(a_s[0])
        for j in range(1, groups):
            bef_s[j] = running
            a_s[j] = jnp.broadcast_to(decay, a_s.shape[1:])
            running = factors[j] * running + r_s[k, behind(j)]
            decay = decay * factors[j]

        @pl.when(seq == 0)
        def _():
            hin_s[k] = jnp.zeros_like(running)

        @pl.when(seq > 0)
        def _():
            h_copy(k).wait_recv()

        incoming = hin_s[k]
        hout_s[k] = decay * incoming + running

        @pl.when(seq < shards - 1)
        def _():
            h_copy(k).start()

        for d in range(1, groups):
            j = ahead(d)
            ps_s[k, d] = a_s[j, 0:1] * incoming + bef_s[j]
            p_copy(k, d).start()
        pr_s[k, 0] = a_s[me, 0:1] * incoming + bef_s[me]

    @pl.loop(0, chunks * groups)
    def _(p):
        k = p // groups
        back = p - k * groups
        d = lax.rem(groups - back, groups)

        @pl.when(back != 0)
        def _():
            p_copy(k, back).wait_recv()

        arriving = pr_s[k, back]
        wide = rows_s[k, d]
        for b in range(blocks):
            low, high = b * BLOCK, (b + 1) * BLOCK
            if b > 0:
                so_far = wide[2 * blocks:2 * blocks + 1]
                for e in range(1, b):
                    so_far = so_far * wide[2 * blocks + e:2 * blocks + e + 1]
                entering = arriving * so_far + m0_s[k, d, b - 1]
            else:
                entering = arriving
            carried = dot3(cm_hi[b], cm_lo[b], entering * wide[b:b + 1])
            out_s[k, d, low:high, :] = out_s[k, d, low:high, :] + carried * go_s[k, d, low:high, :]
        if exact:
            out_copy(k, d).start()
        else:
            @pl.when(column(ahead(d), k) < width)
            def _():
                out_copy(k, d).start()

    for d in range(1, groups):
        t_copy(d).wait_send()

    @pl.loop(0, chunks)
    def _(k):
        @pl.when(seq < shards - 1)
        def _():
            h_copy(k).wait_send()

        for d in range(groups):
            if d > 0:
                m_copy(k, d).wait_send()
                p_copy(k, d).wait_send()
            if exact:
                out_copy(k, d).wait()
            else:
                @pl.when(column(ahead(d), k) < width)
                def _():
                    out_copy(k, d).wait()


def on_device(groups, shards, inputs, log_decay, input_map, output_map, skip_gain):
    tokens, width = inputs.shape
    heads = skip_gain.shape[0]
    state = input_map.shape[1]
    blocks = tokens // BLOCK
    chunks, piece = piece_plan(width, groups)
    row_count = -(-(3 * blocks + 1) // 16) * 16
    kept = -(-(3 * blocks + 1) // 8) * 8
    vmem = pltpu.VMEM
    dma = pltpu.SemaphoreType.DMA
    pieces = (chunks, groups)
    return pl.pallas_call(
        functools.partial(kernel, groups, shards, chunks, piece, width // heads),
        out_shape=jax.ShapeDtypeStruct((tokens, width), F32),
        in_specs=[pl.BlockSpec(memory_space=pl.ANY)] + [pl.BlockSpec(memory_space=vmem)] * 4,
        out_specs=pl.BlockSpec(memory_space=pl.ANY),
        scratch_shapes=[
            vmem(pieces + (tokens, piece), F32),
            vmem(pieces + (tokens, piece), F32),
            vmem(pieces + (tokens, piece), F32),
            vmem(pieces + (max(1, blocks - 1), state, piece), F32),
            vmem(pieces + (state, piece), F32),
            vmem(pieces + (state, piece), F32),
            vmem(pieces + (state, piece), F32),
            vmem(pieces + (state, piece), F32),
            vmem((chunks, state, piece), F32),
            vmem((chunks, state, piece), F32),
            vmem((groups, state, piece), F32),
            vmem((groups, 8, piece), F32),
            vmem(pieces + (kept, piece), F32),
            vmem((blocks, BLOCK + state, BLOCK), BF16),
            vmem((blocks, BLOCK + state, BLOCK), BF16),
            vmem((blocks, BLOCK, state), BF16),
            vmem((blocks, BLOCK, state), BF16),
            vmem((tokens, heads), BF16),
            vmem((tokens, heads), BF16),
            vmem((tokens, heads), BF16),
            vmem((tokens, heads), BF16),
            vmem((row_count, heads), BF16),
            vmem((row_count, heads), BF16),
            vmem((row_count, heads), BF16),
            vmem((8, LANES), F32),
            vmem((groups, 8, LANES), F32),
            dma(pieces), dma(pieces), dma(pieces), dma(pieces), dma(pieces), dma(pieces),
            dma((chunks,)), dma((chunks,)), dma((groups,)), dma((groups,)),
        ],
        compiler_params=pltpu.CompilerParams(
            collective_id=0, has_side_effects=True, vmem_limit_bytes=60 * 1024 * 1024),
    )(inputs, log_decay, input_map, output_map, skip_gain.reshape(1, heads))


def solution(mesh):
    rows = P(("seq", "head"), None)
    body = functools.partial(on_device, mesh.shape["head"], mesh.shape["seq"])
    return jax.shard_map(
        body, mesh=mesh, in_specs=(rows, rows, rows, rows, P()), out_specs=rows, check_vma=False
    )
```

time: 321 us -> 74 us (0.23)
  the two profiles are of different devices: /device:TPU:10 before, /device:TPU:0 now
where the time goes in v1:
time: 74 us; the launch traced here: 73.8 us
  Pallas kernels  66.7 us (90%)
  local copies, waits for them, and re-layouts  7.05 us (10%)
    pallas_call x1, Pallas kernels, on_device(): pl.pallas_call(functools.partial(kernel, groups, shards, chunks, piece, w...  66.7 us
    unnamed x2, local copies, waits for them, and re-layouts  7.05 us

profile of v1, /device:TPU:0, one launch (start us, length us, event | category | flops | bytes accessed | tf_op | source)
XLA Modules:
  0.0 73.8 jit_solution(2333646951142159185)
XLA Ops:
  0.0 1.6 %copy.6.d_ref = f32[256,80]{1,0:T(8,128)} copy(f32[256,80]{0,1:T(8,128)} %param.6) | data formatting | bytes 163840 | tf_op args[1]
  1.6 66.7 %shard_map.55 = f32[256,5120]{1,0:T(8,128)} custom-call(f32[256,5120]{1,0:T(8,128)} %x_hbm.1, f32[256,80]{1,0:T(8,128)} %copy.6.d_ref, f32[256,128]{1,0:T(8,128)} %b_ref.1, f32[256,128]{1,0:T(8,128)} %c_ref.1, f32[1,80]{1,0:T(1,128)} %bitcast.1), custom_call_target="tpu_custom_call" | custom-call | tf_op jit(solution)/shard_map/pallas_call | solution.py:293
  68.4 5.4 %copy.8 = f32[256,5120]{1,0:T(8,128)} copy(f32[256,5120]{1,0:T(8,128)} %shard_map.55) | data formatting | bytes 10485760
